TPU v7x, 256 devices: a whole 4x4x8 slice. The times are simulated.
256 devices in a mesh: gx: 8 (over x, core), gy: 4 (over z_lo), gz: 8 (over y, z_hi).
Axes of the slice: x: 4, y: 4, z: 8 (z_hi: 2, z_lo: 4; z = z_hi * 4 + z_lo), core: 2. Of those that a mesh axis runs over, the one named last changes fastest.
Arguments:
- start_block: float32 [32, 3, 2, 8, 16, 1024], P(None, None, None, 'gx', 'gy', 'gz'), may hold values from -700 to 700
- pair_blocks: float32 [3, 3, 16, 2, 8, 16, 1024], P(None, None, None, None, 'gx', 'gy', 'gz'), may hold values from -8 to 8, as said below
- slot_map: int32 [16, 2, 8, 16, 1024], P(None, None, 'gx', 'gy', 'gz'), may hold values from 0 to 15, as said below
Outputs:
- alpha1: float32 [32, 32], replicated
- alpha2: float32 [32, 32], replicated
- beta1: float32 [32, 32], replicated
- beta2: float32 [32, 32], replicated
- basis3: float32 [32, 3, 2, 8, 16, 1024], P(None, None, None, 'gx', 'gy', 'gz')
Inputs may be any that keep to these rules, and one draw needn't show every extreme that they name: `slot_map`: for every atom the 16 slots hold each of 0 to 15 once; 0 to 13 name the neighbour directions of the steps, 14 and 15 mark padding slots. `pair_blocks`: the block an atom holds toward a neighbour is the transpose of the block that neighbour holds toward the atom, so H is symmetric.
All inputs are finite; a program needn't handle non-finite values.
Results may differ from a plain program's by a relative error of at most 0.0003.
Values sent between devices are 32-bit elements; how exact they have to be, the bound alone decides.
A program may use at most 64 MiB of HBM per device.

v0:
```python
import jax
import jax.numpy as jnp
from jax import lax
from jax.sharding import PartitionSpec as P

PRECISE = lax.Precision.HIGHEST


def extended(block, sides, width):
    for axis, dim in sides:
        count = lax.axis_size(axis)
        forward = [(i, i + 1) for i in range(count - 1)]
        forward.append((count - 1, 0))
        backward = [(target, source) for source, target in forward]
        low = lax.ppermute(
            lax.slice_in_dim(block, block.shape[dim] - width, None, axis=dim), axis, forward
        )
        high = lax.ppermute(lax.slice_in_dim(block, 0, width, axis=dim), axis, backward)
        block = jnp.concatenate([low, block, high], axis=dim)
    return block


def neighbour_offset(sublattice, offset_id):
    if offset_id < 8:
        corner_bits = (offset_id >> 2 & 1, offset_id >> 1 & 1, offset_id & 1)
        if sublattice == 0:
            return ((-corner_bits[0], -corner_bits[1], -corner_bits[2]), 1)
        return (corner_bits, 0)
    axis_id = (offset_id - 8) // 2
    direction = 1 if (offset_id - 8) % 2 == 0 else -1
    displacement = tuple((direction if axis_number == axis_id else 0 for axis_number in range(3)))
    return (displacement, sublattice)


def offset_blocks(pair_blocks, slot_map):
    result = []
    for offset_id in range(14):
        chosen = slot_map[None, None] == offset_id
        result.append(jnp.sum(jnp.where(chosen, pair_blocks, jnp.float32(0.0)), axis=2))
    return result


def onsite_blocks(blocks):
    result = []
    for sublattice in range(2):
        onsite = jnp.zeros(blocks[0].shape[:2] + blocks[0].shape[3:], jnp.float32)
        for offset_id in range(14):
            coupling = blocks[offset_id][:, :, sublattice]
            onsite = onsite + 0.5 * (coupling + jnp.swapaxes(coupling, 0, 1))
        result.append(onsite)
    return result


def apply_hessian(vectors, blocks, onsite):
    padded = extended(vectors, (("gx", 3), ("gy", 4), ("gz", 5)), 1)
    size_x, size_y, size_z = (vectors.shape[3], vectors.shape[4], vectors.shape[5])
    outputs = []
    for sublattice in range(2):
        summed = jnp.zeros(vectors.shape[:2] + vectors.shape[3:], jnp.float32)
        for offset_id in range(14):
            displacement, source = neighbour_offset(sublattice, offset_id)
            start_x = 1 + displacement[0]
            start_y = 1 + displacement[1]
            start_z = 1 + displacement[2]
            neighbour = padded[
                :,
                :,
                source,
                start_x : start_x + size_x,
                start_y : start_y + size_y,
                start_z : start_z + size_z,
            ]
            coupling = blocks[offset_id][:, :, sublattice]
            summed = summed + jnp.sum(coupling[None] * neighbour[:, None], axis=2)
        summed = summed - jnp.sum(
            onsite[sublattice][None] * vectors[:, None, :, sublattice], axis=2
        )
        outputs.append(summed)
    return jnp.stack(outputs, axis=2)


def local_gram(left, right):
    left_flat = left.reshape(left.shape[0], -1)
    right_flat = right.reshape(right.shape[0], -1)
    return lax.dot_general(left_flat, right_flat, (((1,), (1,)), ((), ())), precision=PRECISE)


def combine(matrix, vectors):
    flat = vectors.reshape(vectors.shape[0], -1)
    return jnp.dot(matrix, flat, precision=PRECISE).reshape(vectors.shape)


def inverse_factor(gram_matrix):
    lower = jnp.linalg.cholesky(gram_matrix)
    identity = jnp.eye(gram_matrix.shape[0], dtype=gram_matrix.dtype)
    inverse = jax.scipy.linalg.solve_triangular(lower, identity, lower=True)
    return (lower, inverse)


def lanczos_step(basis, image, previous, coupling_prev, row_count):
    alpha = lax.psum(local_gram(image, basis), ("gx", "gy", "gz")) / row_count
    residual = image - combine(alpha, basis)
    if previous is not None:
        residual = residual - combine(coupling_prev.T, previous)
    residual_gram = lax.psum(local_gram(residual, residual), ("gx", "gy", "gz")) / row_count
    return (alpha, residual, residual_gram)


def local(start_block, pair_blocks, slot_map):
    device_count = lax.axis_size("gx") * lax.axis_size("gy") * lax.axis_size("gz")
    row_count = start_block[0].size * device_count
    blocks = offset_blocks(pair_blocks, slot_map)
    onsite = onsite_blocks(blocks)
    start_gram = lax.psum(local_gram(start_block, start_block), ("gx", "gy", "gz")) / row_count
    lower0, inverse0 = inverse_factor(start_gram)
    basis1 = combine(inverse0, start_block)
    image1 = apply_hessian(basis1, blocks, onsite)
    alpha1, residual1, gram_first = lanczos_step(basis1, image1, None, None, row_count)
    beta1, inverse1 = inverse_factor(gram_first)
    basis2 = combine(inverse1, residual1)
    image2 = apply_hessian(basis2, blocks, onsite)
    alpha2, residual2, gram_second = lanczos_step(basis2, image2, basis1, beta1, row_count)
    beta2, inverse2 = inverse_factor(gram_second)
    basis3 = combine(inverse2, residual2)
    return (alpha1, alpha2, beta1, beta2, basis3)


def solution(mesh):
    in_specs = (
        P(None, None, None, "gx", "gy", "gz"),
        P(None, None, None, None, "gx", "gy", "gz"),
        P(None, None, "gx", "gy", "gz"),
    )
    out_specs = (P(), P(), P(), P(), P(None, None, None, "gx", "gy", "gz"))
    return jax.shard_map(local, mesh=mesh, in_specs=in_specs, out_specs=out_specs, check_vma=False)
```

profile of v0, /device:TPU:1, one launch (start us, length us, event | category | flops | bytes accessed | tf_op | source)
XLA Modules:
  0.0 522.5 jit_solution(3226206658296597986)
XLA Ops:
  3.4 81.5 %psum.35 = f32[32,32]{0,1:T(8,128)S(1)} all-reduce(f32[32,32]{0,1:T(8,128)S(1)} %convolution_bitcast_fusion.2), channel_id=1, replica_groups=mesh['gx'=8,'gy'=4,'gz'=8] {'gx','gy','gz'}, use_global_device_ids=true, to_apply=%region_1.2 | all-reduce | flops 1024 | bytes 8192 | tf_op jit(solution)/shard_map/psum | solution.py:114
  85.0 2.9 cholesky.59
  89.3 2.4 custom-call.7
  94.1 2.5 select_reduce_fusion.13
  106.4 2.7 collective-permute-start.3
  113.4 6.9 %collective-permute-done.3 = f32[32,3,2,3,1,128]{5,0,4,3,2,1:T(8,128)S(1)} collective-permute-done((f32[32,3,2,3,1,128]{5,0,4,3,2,1:T(8,128)S(1)}, f32[32,3,2,3,1,128]{5,0,4,3,2,1:T(8,128)S(1)}, u32[]{:S(2)}, u32[]{:S(2)}) %collective-permute-start.3) | collective-permute-done | bytes 294944 | tf_op jit(solution)/shard_map/ppermute | solution.py:18
  123.1 2.8 copy.507
  125.9 5.6 %collective-permute-start.5 = (f32[32,3,2,3,6,1]{0,2,5,4,3,1:T(2,128)}, f32[32,3,2,3,6,1]{0,2,5,4,3,1:T(2,128)}, u32[]{:S(2)}, u32[]{:S(2)}) collective-permute-start(f32[32,3,2,3,6,1]{0,2,5,4,3,1:T(2,128)} %copy.507), channel_id=1, source_target_pairs={{1,0},{2,1},{3,2},{4,3},{5,4},{6,5},{7,6},{0,7},{9,8},{10,9},{11,1... | collective-permute-start | bytes 41480 | tf_op jit(solution)/shard_map/ppermute | solution.py:18
  134.5 2.7 copy.419
  137.2 5.0 collective-permute-done.4
  151.0 74.3 %psum.36 = f32[32,32]{0,1:T(8,128)S(1)} all-reduce(f32[32,32]{0,1:T(8,128)S(1)} %fusion.56), channel_id=1, replica_groups=mesh['gx'=8,'gy'=4,'gz'=8] {'gx','gy','gz'}, use_global_device_ids=true, to_apply=%region_47.50 | all-reduce | flops 1024 | bytes 8192 | tf_op jit(solution)/shard_map/psum | solution.py:101
  226.4 73.7 %psum.37 = f32[32,32]{0,1:T(8,128)S(1)} all-reduce(f32[32,32]{0,1:T(8,128)S(1)} %fusion.57), channel_id=1, replica_groups=mesh['gx'=8,'gy'=4,'gz'=8] {'gx','gy','gz'}, use_global_device_ids=true, to_apply=%region_48.51 | all-reduce | flops 1024 | bytes 8192 | tf_op jit(solution)/shard_map/psum | solution.py:105
  300.2 2.9 cholesky.70
  304.4 2.4 custom-call.8
  314.0 2.6 collective-permute-done.7
  322.6 4.1 collective-permute-done.8
  326.7 5.3 %collective-permute-done.9 = f32[32,3,2,3,1,128]{5,0,4,3,2,1:T(8,128)S(1)} collective-permute-done((f32[32,3,2,3,1,128]{5,0,4,3,2,1:T(8,128)S(1)}, f32[32,3,2,3,1,128]{5,0,4,3,2,1:T(8,128)S(1)}, u32[]{:S(2)}, u32[]{:S(2)}) %collective-permute-start.9) | collective-permute-done | bytes 294944 | tf_op jit(solution)/shard_map/ppermute | solution.py:18
  334.8 2.8 copy.509
  337.6 4.7 collective-permute-start.11
  350.4 4.6 collective-permute-done.10
  363.7 73.7 %psum.38 = f32[32,32]{0,1:T(8,128)S(1)} all-reduce(f32[32,32]{0,1:T(8,128)S(1)} %fusion.59), channel_id=1, replica_groups=mesh['gx'=8,'gy'=4,'gz'=8] {'gx','gy','gz'}, use_global_device_ids=true, to_apply=%region_79.82 | all-reduce | flops 1024 | bytes 8192 | tf_op jit(solution)/shard_map/psum | solution.py:101
  439.1 73.7 %psum.39 = f32[32,32]{0,1:T(8,128)S(1)} all-reduce(f32[32,32]{0,1:T(8,128)S(1)} %fusion.60), channel_id=1, replica_groups=mesh['gx'=8,'gy'=4,'gz'=8] {'gx','gy','gz'}, use_global_device_ids=true, to_apply=%region_80.83 | all-reduce | flops 1024 | bytes 8192 | tf_op jit(solution)/shard_map/psum | solution.py:105
  512.8 2.9 cholesky.81
  517.6 2.4 custom-call.9
  (361 shorter events, 74.9 us)
Async XLA Ops:
  3.4 90.4 %copy-start.95 = (s32[16,2,1,4,128]{4,3,2,1,0:T(4,128)S(1)}, s32[16,2,1,4,128]{4,3,2,1,0:T(4,128)}, u32[]{:S(2)}) copy-start(s32[16,2,1,4,128]{4,3,2,1,0:T(4,128)} %param.8) | copy-start | bytes 196612
  88.6 5.5 %copy-start.35 = (f32[3,3,16,2,1,4,128]{6,5,4,3,2,1,0:T(4,128)S(1)}, f32[3,3,16,2,1,4,128]{6,5,4,3,2,1,0:T(4,128)}, u32[]{:S(2)}) copy-start(f32[3,3,16,2,1,4,128]{6,5,4,3,2,1,0:T(4,128)} %param.7) | copy-start | bytes 1769476
  92.8 12.8 %collective-permute-start = (f32[32,3,2,1,4,128]{5,0,4,3,2,1:T(8,128)S(1)}, f32[32,3,2,1,4,128]{5,0,4,3,2,1:T(8,128)S(1)}, u32[]{:S(2)}, u32[]{:S(2)}) collective-permute-start(f32[32,3,2,1,4,128]{5,0,4,3,2,1:T(8,128)S(1)} %copy.391), channel_id=1, source_target_pairs={{0,32},{32,64},{64,96},{96,128},{128,160},{160,192},{192,224},{224... | collective-permute-start | bytes 1179656 | tf_op jit(solution)/shard_map/ppermute | solution.py:15
  92.8 12.9 %collective-permute-start.1 = (f32[32,3,2,1,4,128]{5,0,4,3,2,1:T(8,128)S(1)}, f32[32,3,2,1,4,128]{5,0,4,3,2,1:T(8,128)S(1)}, u32[]{:S(2)}, u32[]{:S(2)}) collective-permute-start(f32[32,3,2,1,4,128]{5,0,4,3,2,1:T(8,128)S(1)} %copy.391), channel_id=1, source_target_pairs={{32,0},{64,32},{96,64},{128,96},{160,128},{192,160},{224,192},{0,2... | collective-permute-start | bytes 1179656 | tf_op jit(solution)/shard_map/ppermute | solution.py:18
  99.9 10.0 %copy-start.84 = (f32[3,3,4,128]{3,2,0,1:T(4,128)}, f32[3,3,4,128]{3,2,0,1:T(4,128)S(1)}, u32[]{:S(2)}) copy-start(f32[3,3,4,128]{3,2,0,1:T(4,128)S(1)} %get-tuple-element.159) | copy-start | bytes 55300
  99.9 10.7 %copy-start.82 = (f32[3,3,4,128]{3,2,0,1:T(4,128)}, f32[3,3,4,128]{3,2,0,1:T(4,128)S(1)}, u32[]{:S(2)}) copy-start(f32[3,3,4,128]{3,2,0,1:T(4,128)S(1)} %get-tuple-element.162) | copy-start | bytes 55300
  100.5 10.9 %copy-start.80 = (f32[3,3,4,128]{3,2,0,1:T(4,128)}, f32[3,3,4,128]{3,2,0,1:T(4,128)S(1)}, u32[]{:S(2)}) copy-start(f32[3,3,4,128]{3,2,0,1:T(4,128)S(1)} %get-tuple-element.194) | copy-start | bytes 55300
  102.5 8.1 %copy-start.88 = (f32[3,3,4,128]{3,2,0,1:T(4,128)}, f32[3,3,4,128]{3,2,0,1:T(4,128)S(1)}, u32[]{:S(2)}) copy-start(f32[3,3,4,128]{3,2,0,1:T(4,128)S(1)} %get-tuple-element.190) | copy-start | bytes 55300
  102.5 9.0 %copy-start.86 = (f32[3,3,4,128]{3,2,0,1:T(4,128)}, f32[3,3,4,128]{3,2,0,1:T(4,128)S(1)}, u32[]{:S(2)}) copy-start(f32[3,3,4,128]{3,2,0,1:T(4,128)S(1)} %get-tuple-element.189) | copy-start | bytes 55300
  105.8 7.6 %collective-permute-start.2 = (f32[32,3,2,3,1,128]{5,0,4,3,2,1:T(8,128)S(1)}, f32[32,3,2,3,1,128]{5,0,4,3,2,1:T(8,128)S(1)}, u32[]{:S(2)}, u32[]{:S(2)}) collective-permute-start(f32[32,3,2,3,1,128]{5,0,4,3,2,1:T(8,128)S(1)} %get-tuple-element.115), channel_id=1, source_target_pairs={{0,8},{8,16},{16,24},{24,0},{1,9},{9,17},{17,25},{25,1},{2,10},{10... | collective-permute-start | bytes 884744 | tf_op jit(solution)/shard_map/ppermute | solution.py:15
  106.4 13.9 %collective-permute-start.3 = (f32[32,3,2,3,1,128]{5,0,4,3,2,1:T(8,128)S(1)}, f32[32,3,2,3,1,128]{5,0,4,3,2,1:T(8,128)S(1)}, u32[]{:S(2)}, u32[]{:S(2)}) collective-permute-start(f32[32,3,2,3,1,128]{5,0,4,3,2,1:T(8,128)S(1)} %get-tuple-element.116), channel_id=1, source_target_pairs={{8,0},{16,8},{24,16},{0,24},{9,1},{17,9},{25,17},{1,25},{10,2},{18... | collective-permute-start | bytes 884744 | tf_op jit(solution)/shard_map/ppermute | solution.py:18
  113.4 6.9 %copy-start.8 = (f32[32,3,2,3,1,128]{5,0,4,3,2,1:T(8,128)}, f32[32,3,2,3,1,128]{5,0,4,3,2,1:T(8,128)S(1)}, u32[]{:S(2)}) copy-start(f32[32,3,2,3,1,128]{5,0,4,3,2,1:T(8,128)S(1)} %collective-permute-done.2) | copy-start | bytes 884740
  125.9 8.6 %collective-permute-start.5 = (f32[32,3,2,3,6,1]{0,2,5,4,3,1:T(2,128)}, f32[32,3,2,3,6,1]{0,2,5,4,3,1:T(2,128)}, u32[]{:S(2)}, u32[]{:S(2)}) collective-permute-start(f32[32,3,2,3,6,1]{0,2,5,4,3,1:T(2,128)} %copy.507), channel_id=1, source_target_pairs={{1,0},{2,1},{3,2},{4,3},{5,4},{6,5},{7,6},{0,7},{9,8},{10,9},{11,1... | collective-permute-start | bytes 41480 | tf_op jit(solution)/shard_map/ppermute | solution.py:18
  132.8 9.4 %collective-permute-start.4 = (f32[32,3,2,3,6,1]{0,2,5,4,3,1:T(2,128)}, f32[32,3,2,3,6,1]{0,2,5,4,3,1:T(2,128)}, u32[]{:S(2)}, u32[]{:S(2)}) collective-permute-start(f32[32,3,2,3,6,1]{0,2,5,4,3,1:T(2,128)} %copy.506), channel_id=1, source_target_pairs={{0,1},{1,2},{2,3},{3,4},{4,5},{5,6},{6,7},{7,0},{8,9},{9,10},{10,1... | collective-permute-start | bytes 41480 | tf_op jit(solution)/shard_map/ppermute | solution.py:15
  304.4 133.4 %copy-start.94 = (f32[32,32]{1,0:T(8,128)}, f32[32,32]{1,0:T(8,128)S(1)}, u32[]{:S(2)}) copy-start(f32[32,32]{1,0:T(8,128)S(1)} %get-tuple-element.76) | copy-start | bytes 12292
  307.9 5.9 %collective-permute-start.6 = (f32[32,3,2,1,4,128]{5,0,4,3,2,1:T(8,128)S(1)}, f32[32,3,2,1,4,128]{5,0,4,3,2,1:T(8,128)S(1)}, u32[]{:S(2)}, u32[]{:S(2)}) collective-permute-start(f32[32,3,2,1,4,128]{5,0,4,3,2,1:T(8,128)S(1)} %copy.482), channel_id=1, source_target_pairs={{0,32},{32,64},{64,96},{96,128},{128,160},{160,192},{192,224},{224... | collective-permute-start | bytes 1179656 | tf_op jit(solution)/shard_map/ppermute | solution.py:15
  309.1 7.5 %collective-permute-start.7 = (f32[32,3,2,1,4,128]{5,0,4,3,2,1:T(8,128)S(1)}, f32[32,3,2,1,4,128]{5,0,4,3,2,1:T(8,128)S(1)}, u32[]{:S(2)}, u32[]{:S(2)}) collective-permute-start(f32[32,3,2,1,4,128]{5,0,4,3,2,1:T(8,128)S(1)} %copy.482), channel_id=1, source_target_pairs={{32,0},{64,32},{96,64},{128,96},{160,128},{192,160},{224,192},{0,2... | collective-permute-start | bytes 1179656 | tf_op jit(solution)/shard_map/ppermute | solution.py:18
  314.0 6.2 %copy-start.85 = (f32[3,3,4,128]{3,2,0,1:T(4,128)S(1)}, f32[3,3,4,128]{3,2,0,1:T(4,128)}, u32[]{:S(2)}) copy-start(f32[3,3,4,128]{3,2,0,1:T(4,128)} %copy-done.84) | copy-start | bytes 55300
  316.7 5.1 copy-start.81
  316.7 10.0 %collective-permute-start.8 = (f32[32,3,2,3,1,128]{5,0,4,3,2,1:T(8,128)S(1)}, f32[32,3,2,3,1,128]{5,0,4,3,2,1:T(8,128)S(1)}, u32[]{:S(2)}, u32[]{:S(2)}) collective-permute-start(f32[32,3,2,3,1,128]{5,0,4,3,2,1:T(8,128)S(1)} %get-tuple-element.113), channel_id=1, source_target_pairs={{0,8},{8,16},{16,24},{24,0},{1,9},{9,17},{17,25},{25,1},{2,10},{10... | collective-permute-start | bytes 884744 | tf_op jit(solution)/shard_map/ppermute | solution.py:15
  317.7 14.3 %collective-permute-start.9 = (f32[32,3,2,3,1,128]{5,0,4,3,2,1:T(8,128)S(1)}, f32[32,3,2,3,1,128]{5,0,4,3,2,1:T(8,128)S(1)}, u32[]{:S(2)}, u32[]{:S(2)}) collective-permute-start(f32[32,3,2,3,1,128]{5,0,4,3,2,1:T(8,128)S(1)} %get-tuple-element.114), channel_id=1, source_target_pairs={{8,0},{16,8},{24,16},{0,24},{9,1},{17,9},{25,17},{1,25},{10,2},{18... | collective-permute-start | bytes 884744 | tf_op jit(solution)/shard_map/ppermute | solution.py:18
  326.7 5.3 %copy-start.4 = (f32[32,3,2,3,1,128]{5,0,4,3,2,1:T(8,128)}, f32[32,3,2,3,1,128]{5,0,4,3,2,1:T(8,128)S(1)}, u32[]{:S(2)}) copy-start(f32[32,3,2,3,1,128]{5,0,4,3,2,1:T(8,128)S(1)} %collective-permute-done.8) | copy-start | bytes 884740
  337.6 8.1 %collective-permute-start.11 = (f32[32,3,2,3,6,1]{0,2,5,4,3,1:T(2,128)}, f32[32,3,2,3,6,1]{0,2,5,4,3,1:T(2,128)}, u32[]{:S(2)}, u32[]{:S(2)}) collective-permute-start(f32[32,3,2,3,6,1]{0,2,5,4,3,1:T(2,128)} %copy.509), channel_id=1, source_target_pairs={{1,0},{2,1},{3,2},{4,3},{5,4},{6,5},{7,6},{0,7},{9,8},{10,9},{11,1... | collective-permute-start | bytes 41480 | tf_op jit(solution)/shard_map/ppermute | solution.py:18
  345.0 9.9 %collective-permute-start.10 = (f32[32,3,2,3,6,1]{0,2,5,4,3,1:T(2,128)}, f32[32,3,2,3,6,1]{0,2,5,4,3,1:T(2,128)}, u32[]{:S(2)}, u32[]{:S(2)}) collective-permute-start(f32[32,3,2,3,6,1]{0,2,5,4,3,1:T(2,128)} %copy.508), channel_id=1, source_target_pairs={{0,1},{1,2},{2,3},{3,4},{4,5},{5,6},{6,7},{7,0},{8,9},{9,10},{10,1... | collective-permute-start | bytes 41480 | tf_op jit(solution)/shard_map/ppermute | solution.py:15
  (84 other events, 111.4 us)
where the time goes:
time: 524 us; the launch traced here: 522 us
  blocking collectives  377 us (72%)
  other arithmetic  45.5 us (9%)
  local copies, waits for them, and re-layouts  39 us (7%)
  waiting for transfers between devices  31.8 us (6%)
  starting transfers between devices  19.9 us (4%)
  matrix products  7.11 us (1%)
    psum x2, blocking collectives, lanczos_step(): alpha = lax.psum(local_gram(image, basis), ('gx', 'gy', 'gz')) / row_count  148 us
    psum x2, blocking collectives, lanczos_step(): lax.psum(local_gram(residual, residual), ('gx', 'gy', 'gz')) / row_count  147 us
    psum x1, blocking collectives, local(): lax.psum(local_gram(start_block, start_block), ('gx', 'gy', 'gz'))  81.5 us
    unnamed x203, local copies, waits for them, and re-layouts  17 us
    ppermute x6, waiting for transfers between devices, extended(): lax.ppermute(lax.slice_in_dim(block, block.shape[dim] - width, None, axis...  17 us
    ppermute x6, starting transfers between devices, extended(): lax.ppermute(lax.slice_in_dim(block, 0, width, axis=dim), axis, backward)  16.3 us
    ppermute x6, waiting for transfers between devices, extended(): lax.ppermute(lax.slice_in_dim(block, 0, width, axis=dim), axis, backward)  14.8 us
    reduce_sum x42, other arithmetic, apply_hessian(): summed = summed + jnp.sum(coupling[None] * neighbour[:, None], axis=2)  12.5 us
  transfers between devices with their start and end apart: 12, of which 8 were waited for; matrix products, arithmetic and copies ran while one was open for 6% of the time, Pallas kernels for 0%

commit v1 on v0

--- a/solution.py
+++ b/solution.py
@@ -2,6 +2,7 @@
 import jax.numpy as jnp
 from jax import lax
 from jax.sharding import PartitionSpec as P
+from jax.lax import psum
 
 PRECISE = lax.Precision.HIGHEST
 
@@ -98,7 +99,15 @@
 
 
 def lanczos_step(basis, image, previous, coupling_prev, row_count):
-    alpha = lax.psum(local_gram(image, basis), ("gx", "gy", "gz")) / row_count
+
+    def edit_the_sectors(z):
+        axis_name = "gx"
+        across = ("gy", "gz")
+        for tick in (across, axis_name):
+            z = psum(z, tick)
+        return z
+
+    alpha = edit_the_sectors(local_gram(image, basis)) / row_count
     residual = image - combine(alpha, basis)
     if previous is not None:
         residual = residual - combine(coupling_prev.T, previous)

time: 524 us -> 759 us (1.45)
  blocking collectives: 377 us -> 612 us
    psum x2 -> x4, blocking collectives: 148 us -> 373 us  [edit_the_sectors(): z = psum(z, tick)]
    psum x2, blocking collectives: 147 us -> 158 us  [lanczos_step(): lax.psum(local_gram(residual, residual), ('gx', 'gy', 'gz')) / row_count]
  transfers between devices with their start and end apart: 12 -> 12, of which waited for: 8 -> 8; matrix products, arithmetic and copies ran while one was open for 6% -> 4% of each run, Pallas kernels for 0% -> 0%
where the time goes in v1:
time: 759 us; the launch traced here: 758 us
  blocking collectives  612 us (81%)
  other arithmetic  45.5 us (6%)
  local copies, waits for them, and re-layouts  39 us (5%)
  waiting for transfers between devices  30.8 us (4%)
  starting transfers between devices  20.5 us (3%)
    psum x4, blocking collectives, edit_the_sectors(): z = psum(z, tick)  373 us
    psum x2, blocking collectives, lanczos_step(): lax.psum(local_gram(residual, residual), ('gx', 'gy', 'gz')) / row_count  158 us
    psum x1, blocking collectives, local(): lax.psum(local_gram(start_block, start_block), ('gx', 'gy', 'gz'))  81.5 us
    unnamed x203, local copies, waits for them, and re-layouts  17 us
    ppermute x6, waiting for transfers between devices, extended(): lax.ppermute(lax.slice_in_dim(block, block.shape[dim] - width, None, axis...  15.8 us
  transfers between devices with their start and end apart: 12, of which 8 were waited for; matrix products, arithmetic and copies ran while one was open for 4% of the time, Pallas kernels for 0%

profile of v1, /device:TPU:1, one launch (start us, length us, event | category | flops | bytes accessed | tf_op | source)
XLA Modules:
  0.0 757.6 jit_solution(3041881404794186468)
XLA Ops:
  3.5 81.5 %psum.49 = f32[32,32]{0,1:T(8,128)S(1)} all-reduce(f32[32,32]{0,1:T(8,128)S(1)} %convolution_bitcast_fusion.2), channel_id=1, replica_groups=mesh['gx'=8,'gy'=4,'gz'=8] {'gx','gy','gz'}, use_global_device_ids=true, to_apply=%region_1.2 | all-reduce | flops 1024 | bytes 8192 | tf_op jit(solution)/shard_map/psum | solution.py:123
  85.1 2.9 cholesky.59
  89.4 2.4 custom-call.7
  94.2 2.5 select_reduce_fusion.13
  106.5 2.7 collective-permute-start.3
  113.5 6.9 collective-permute-done.3
  123.1 2.8 copy.507
  125.9 5.6 collective-permute-start.5
  134.5 2.7 copy.419
  137.2 5.0 collective-permute-done.4
  151.1 136.6 %psum.50 = f32[32,32]{0,1:T(8,128)S(1)} all-reduce(f32[32,32]{0,1:T(8,128)S(1)} %fusion.56), channel_id=1, replica_groups=mesh['gx'=8,'gy'=4,'gz'=8] {'gy','gz'}, use_global_device_ids=true, to_apply=%region_47.50 | all-reduce | flops 1024 | bytes 8192 | tf_op jit(solution)/shard_map/psum | solution.py:107
  287.7 49.5 %psum.51 = f32[32,32]{0,1:T(8,128)S(1)} all-reduce(f32[32,32]{0,1:T(8,128)S(1)} %psum.50), channel_id=1, replica_groups=mesh['gx'=8,'gy'=4,'gz'=8] {'gx'}, use_global_device_ids=true, to_apply=%region_48.51 | all-reduce | flops 1024 | bytes 8192 | tf_op jit(solution)/shard_map/psum | solution.py:107
  338.3 78.8 %psum.52 = f32[32,32]{0,1:T(8,128)S(1)} all-reduce(f32[32,32]{0,1:T(8,128)S(1)} %fusion.57), channel_id=1, replica_groups=mesh['gx'=8,'gy'=4,'gz'=8] {'gx','gy','gz'}, use_global_device_ids=true, to_apply=%region_49.52 | all-reduce | flops 1024 | bytes 8192 | tf_op jit(solution)/shard_map/psum | solution.py:114
  417.1 2.9 cholesky.70
  421.4 2.4 custom-call.8
  439.9 4.5 collective-permute-done.8
  444.3 5.7 collective-permute-done.9
  452.9 2.8 copy.509
  455.6 3.7 collective-permute-start.11
  468.5 3.0 collective-permute-done.10
  480.2 137.0 %psum.53 = f32[32,32]{0,1:T(8,128)S(1)} all-reduce(f32[32,32]{0,1:T(8,128)S(1)} %fusion.59), channel_id=1, replica_groups=mesh['gx'=8,'gy'=4,'gz'=8] {'gy','gz'}, use_global_device_ids=true, to_apply=%region_80.83 | all-reduce | flops 1024 | bytes 8192 | tf_op jit(solution)/shard_map/psum | solution.py:107
  617.2 49.7 %psum.54 = f32[32,32]{0,1:T(8,128)S(1)} all-reduce(f32[32,32]{0,1:T(8,128)S(1)} %psum.53), channel_id=1, replica_groups=mesh['gx'=8,'gy'=4,'gz'=8] {'gx'}, use_global_device_ids=true, to_apply=%region_81.84 | all-reduce | flops 1024 | bytes 8192 | tf_op jit(solution)/shard_map/psum | solution.py:107
  668.6 79.2 %psum.55 = f32[32,32]{0,1:T(8,128)S(1)} all-reduce(f32[32,32]{0,1:T(8,128)S(1)} %fusion.60), channel_id=1, replica_groups=mesh['gx'=8,'gy'=4,'gz'=8] {'gx','gy','gz'}, use_global_device_ids=true, to_apply=%region_82.85 | all-reduce | flops 1024 | bytes 8192 | tf_op jit(solution)/shard_map/psum | solution.py:114
  747.9 2.9 cholesky.81
  (363 shorter events, 81.4 us)
Async XLA Ops:
  3.5 90.4 %copy-start.95 = (s32[16,2,1,4,128]{4,3,2,1,0:T(4,128)S(1)}, s32[16,2,1,4,128]{4,3,2,1,0:T(4,128)}, u32[]{:S(2)}) copy-start(s32[16,2,1,4,128]{4,3,2,1,0:T(4,128)} %param.8) | copy-start | bytes 196612
  88.7 5.5 copy-start.35
  92.8 12.8 %collective-permute-start = (f32[32,3,2,1,4,128]{5,0,4,3,2,1:T(8,128)S(1)}, f32[32,3,2,1,4,128]{5,0,4,3,2,1:T(8,128)S(1)}, u32[]{:S(2)}, u32[]{:S(2)}) collective-permute-start(f32[32,3,2,1,4,128]{5,0,4,3,2,1:T(8,128)S(1)} %copy.391), channel_id=1, source_target_pairs={{0,32},{32,64},{64,96},{96,128},{128,160},{160,192},{192,224},{224... | collective-permute-start | bytes 1179656 | tf_op jit(solution)/shard_map/ppermute | solution.py:16
  92.8 12.9 %collective-permute-start.1 = (f32[32,3,2,1,4,128]{5,0,4,3,2,1:T(8,128)S(1)}, f32[32,3,2,1,4,128]{5,0,4,3,2,1:T(8,128)S(1)}, u32[]{:S(2)}, u32[]{:S(2)}) collective-permute-start(f32[32,3,2,1,4,128]{5,0,4,3,2,1:T(8,128)S(1)} %copy.391), channel_id=1, source_target_pairs={{32,0},{64,32},{96,64},{128,96},{160,128},{192,160},{224,192},{0,2... | collective-permute-start | bytes 1179656 | tf_op jit(solution)/shard_map/ppermute | solution.py:19
  99.9 10.0 %copy-start.84 = (f32[3,3,4,128]{3,2,0,1:T(4,128)}, f32[3,3,4,128]{3,2,0,1:T(4,128)S(1)}, u32[]{:S(2)}) copy-start(f32[3,3,4,128]{3,2,0,1:T(4,128)S(1)} %get-tuple-element.159) | copy-start | bytes 55300
  99.9 10.7 %copy-start.82 = (f32[3,3,4,128]{3,2,0,1:T(4,128)}, f32[3,3,4,128]{3,2,0,1:T(4,128)S(1)}, u32[]{:S(2)}) copy-start(f32[3,3,4,128]{3,2,0,1:T(4,128)S(1)} %get-tuple-element.162) | copy-start | bytes 55300
  100.6 10.9 %copy-start.80 = (f32[3,3,4,128]{3,2,0,1:T(4,128)}, f32[3,3,4,128]{3,2,0,1:T(4,128)S(1)}, u32[]{:S(2)}) copy-start(f32[3,3,4,128]{3,2,0,1:T(4,128)S(1)} %get-tuple-element.194) | copy-start | bytes 55300
  102.5 8.1 %copy-start.88 = (f32[3,3,4,128]{3,2,0,1:T(4,128)}, f32[3,3,4,128]{3,2,0,1:T(4,128)S(1)}, u32[]{:S(2)}) copy-start(f32[3,3,4,128]{3,2,0,1:T(4,128)S(1)} %get-tuple-element.190) | copy-start | bytes 55300
  102.5 9.0 %copy-start.86 = (f32[3,3,4,128]{3,2,0,1:T(4,128)}, f32[3,3,4,128]{3,2,0,1:T(4,128)S(1)}, u32[]{:S(2)}) copy-start(f32[3,3,4,128]{3,2,0,1:T(4,128)S(1)} %get-tuple-element.189) | copy-start | bytes 55300
  105.8 7.6 %collective-permute-start.2 = (f32[32,3,2,3,1,128]{5,0,4,3,2,1:T(8,128)S(1)}, f32[32,3,2,3,1,128]{5,0,4,3,2,1:T(8,128)S(1)}, u32[]{:S(2)}, u32[]{:S(2)}) collective-permute-start(f32[32,3,2,3,1,128]{5,0,4,3,2,1:T(8,128)S(1)} %get-tuple-element.115), channel_id=1, source_target_pairs={{0,8},{8,16},{16,24},{24,0},{1,9},{9,17},{17,25},{25,1},{2,10},{10... | collective-permute-start | bytes 884744 | tf_op jit(solution)/shard_map/ppermute | solution.py:16
  106.5 13.9 %collective-permute-start.3 = (f32[32,3,2,3,1,128]{5,0,4,3,2,1:T(8,128)S(1)}, f32[32,3,2,3,1,128]{5,0,4,3,2,1:T(8,128)S(1)}, u32[]{:S(2)}, u32[]{:S(2)}) collective-permute-start(f32[32,3,2,3,1,128]{5,0,4,3,2,1:T(8,128)S(1)} %get-tuple-element.116), channel_id=1, source_target_pairs={{8,0},{16,8},{24,16},{0,24},{9,1},{17,9},{25,17},{1,25},{10,2},{18... | collective-permute-start | bytes 884744 | tf_op jit(solution)/shard_map/ppermute | solution.py:19
  113.4 6.9 copy-start.8
  125.9 8.6 %collective-permute-start.5 = (f32[32,3,2,3,6,1]{0,2,5,4,3,1:T(2,128)}, f32[32,3,2,3,6,1]{0,2,5,4,3,1:T(2,128)}, u32[]{:S(2)}, u32[]{:S(2)}) collective-permute-start(f32[32,3,2,3,6,1]{0,2,5,4,3,1:T(2,128)} %copy.507), channel_id=1, source_target_pairs={{1,0},{2,1},{3,2},{4,3},{5,4},{6,5},{7,6},{0,7},{9,8},{10,9},{11,1... | collective-permute-start | bytes 41480 | tf_op jit(solution)/shard_map/ppermute | solution.py:19
  132.8 9.4 %collective-permute-start.4 = (f32[32,3,2,3,6,1]{0,2,5,4,3,1:T(2,128)}, f32[32,3,2,3,6,1]{0,2,5,4,3,1:T(2,128)}, u32[]{:S(2)}, u32[]{:S(2)}) collective-permute-start(f32[32,3,2,3,6,1]{0,2,5,4,3,1:T(2,128)} %copy.506), channel_id=1, source_target_pairs={{0,1},{1,2},{2,3},{3,4},{4,5},{5,6},{6,7},{7,0},{8,9},{9,10},{10,1... | collective-permute-start | bytes 41480 | tf_op jit(solution)/shard_map/ppermute | solution.py:16
  421.4 246.0 %copy-start.94 = (f32[32,32]{1,0:T(8,128)}, f32[32,32]{1,0:T(8,128)S(1)}, u32[]{:S(2)}) copy-start(f32[32,32]{1,0:T(8,128)S(1)} %get-tuple-element.76) | copy-start | bytes 12292
  424.9 6.5 collective-permute-start.6
  426.7 7.2 collective-permute-start.7
  431.5 5.9 copy-start.85
  433.9 5.1 copy-start.81
  434.0 10.3 %collective-permute-start.8 = (f32[32,3,2,3,1,128]{5,0,4,3,2,1:T(8,128)S(1)}, f32[32,3,2,3,1,128]{5,0,4,3,2,1:T(8,128)S(1)}, u32[]{:S(2)}, u32[]{:S(2)}) collective-permute-start(f32[32,3,2,3,1,128]{5,0,4,3,2,1:T(8,128)S(1)} %get-tuple-element.113), channel_id=1, source_target_pairs={{0,8},{8,16},{16,24},{24,0},{1,9},{9,17},{17,25},{25,1},{2,10},{10... | collective-permute-start | bytes 884744 | tf_op jit(solution)/shard_map/ppermute | solution.py:16
  435.4 14.7 %collective-permute-start.9 = (f32[32,3,2,3,1,128]{5,0,4,3,2,1:T(8,128)S(1)}, f32[32,3,2,3,1,128]{5,0,4,3,2,1:T(8,128)S(1)}, u32[]{:S(2)}, u32[]{:S(2)}) collective-permute-start(f32[32,3,2,3,1,128]{5,0,4,3,2,1:T(8,128)S(1)} %get-tuple-element.114), channel_id=1, source_target_pairs={{8,0},{16,8},{24,16},{0,24},{9,1},{17,9},{25,17},{1,25},{10,2},{18... | collective-permute-start | bytes 884744 | tf_op jit(solution)/shard_map/ppermute | solution.py:19
  444.3 5.7 copy-start.4
  455.6 8.1 %collective-permute-start.11 = (f32[32,3,2,3,6,1]{0,2,5,4,3,1:T(2,128)}, f32[32,3,2,3,6,1]{0,2,5,4,3,1:T(2,128)}, u32[]{:S(2)}, u32[]{:S(2)}) collective-permute-start(f32[32,3,2,3,6,1]{0,2,5,4,3,1:T(2,128)} %copy.509), channel_id=1, source_target_pairs={{1,0},{2,1},{3,2},{4,3},{5,4},{6,5},{7,6},{0,7},{9,8},{10,9},{11,1... | collective-permute-start | bytes 41480 | tf_op jit(solution)/shard_map/ppermute | solution.py:19
  462.1 9.4 %collective-permute-start.10 = (f32[32,3,2,3,6,1]{0,2,5,4,3,1:T(2,128)}, f32[32,3,2,3,6,1]{0,2,5,4,3,1:T(2,128)}, u32[]{:S(2)}, u32[]{:S(2)}) collective-permute-start(f32[32,3,2,3,6,1]{0,2,5,4,3,1:T(2,128)} %copy.508), channel_id=1, source_target_pairs={{0,1},{1,2},{2,3},{3,4},{4,5},{5,6},{6,7},{7,0},{8,9},{9,10},{10,1... | collective-permute-start | bytes 41480 | tf_op jit(solution)/shard_map/ppermute | solution.py:16
  (84 other events, 114.4 us)
